TPU v7x, 128 devices: a whole 4x4x4 slice. The times are simulated.
128 devices in a mesh: section: 2 (over core), cin: 8 (over z_hi, y), cout: 8 (over z_lo, x).
Axes of the slice: x: 4, y: 4, z: 4 (z_hi: 2, z_lo: 2; z = z_hi * 2 + z_lo), core: 2. Of those that a mesh axis runs over, the one named last changes fastest.
Arguments:
- inner_features: bfloat16 [2, 784, 2560], P('section', None, ('cin', 'cout')), may hold values from 0 to 2
- block_input: bfloat16 [2, 784, 5120], P('section', None, ('cin', 'cout')), may hold values from -6 to 6
- first_kernel: bfloat16 [9, 2560, 2560], P(None, 'cin', 'cout'), may hold values from -0.0546875 to 0.0546875
- expand_weight: bfloat16 [2560, 5120], P('cout', 'cin'), may hold values from -0.15625 to 0.15625
- reduce_weight: bfloat16 [5120, 5120], P(('cin', 'section'), 'cout'), may hold values from -0.125 to 0.125
- stride_kernel: bfloat16 [9, 5120, 5120], P(None, 'cout', ('section', 'cin')), may hold values from -0.0390625 to 0.0390625
- output_grad: bfloat16 [2, 196, 5120], P(None, None, ('section', 'cin', 'cout')), may hold values from -6 to 6
Outputs:
- inner_gradient: float32 [2, 784, 2560], P('section', None, ('cin', 'cout'))
- input_gradient: bfloat16 [2, 784, 5120], P('section', None, ('cin', 'cout'))
- first_gradient: float32 [9, 2560, 2560], P(None, 'cin', 'cout')
- expand_gradient: float32 [2560, 5120], P('cout', 'cin')
- reduce_gradient: float32 [5120, 5120], P(('cin', 'section'), 'cout')
- stride_gradient: float32 [9, 5120, 5120], P(None, 'cout', ('section', 'cin'))
All inputs are finite; a program needn't handle non-finite values.
Results may differ from a plain program's by a relative error of at most 0.013.
Values may be sent and summed in bfloat16 or wider, within the bound.
A program may use at most 192 MiB of HBM per device.

v0:
```python
import jax
import jax.numpy as jnp
from jax import lax
from jax.sharding import PartitionSpec as P

SIDE = 28


def smooth_gate(values):
    return values * jax.nn.sigmoid(values)


def gate_slope(values):
    logistic = jax.nn.sigmoid(values)
    return logistic * (1.0 + values * (1.0 - logistic))


def flatten_rows(images):
    return images.reshape(images.shape[0] * images.shape[1], images.shape[2])


def project(images, matrix):
    product = jnp.dot(flatten_rows(images), matrix, preferred_element_type=jnp.float32)
    return product.reshape(images.shape[0], images.shape[1], matrix.shape[1])


def project_back(grads, matrix):
    product = lax.dot_general(
        flatten_rows(grads), matrix, (((1,), (1,)), ((), ())), preferred_element_type=jnp.float32
    )
    return product.reshape(grads.shape[0], grads.shape[1], matrix.shape[0])


def outer_rows(left, right):
    return lax.dot_general(
        flatten_rows(left),
        flatten_rows(right),
        (((0,), (0,)), ((), ())),
        preferred_element_type=jnp.float32,
    )


def padded_grid(images, side):
    grid = images.reshape(images.shape[0], side, side, images.shape[2])
    return jnp.pad(grid, ((0, 0), (1, 1), (1, 1), (0, 0)))


def conv_same(images, kernel, side):
    padded = padded_grid(images, side)
    total = jnp.zeros((images.shape[0] * side * side, kernel.shape[2]), jnp.float32)
    for row in range(3):
        for column in range(3):
            window = padded[:, row : row + side, column : column + side, :].reshape(
                -1, images.shape[2]
            )
            total = total + jnp.dot(
                window, kernel[3 * row + column], preferred_element_type=jnp.float32
            )
    return total.reshape(images.shape[0], side * side, kernel.shape[2])


def conv_same_back(grads, kernel, side):
    padded = padded_grid(grads, side)
    total = jnp.zeros((grads.shape[0] * side * side, kernel.shape[1]), jnp.float32)
    for row in range(3):
        for column in range(3):
            window = padded[:, 2 - row : 2 - row + side, 2 - column : 2 - column + side, :].reshape(
                -1, grads.shape[2]
            )
            total = total + lax.dot_general(
                window,
                kernel[3 * row + column],
                (((1,), (1,)), ((), ())),
                preferred_element_type=jnp.float32,
            )
    return total.reshape(grads.shape[0], side * side, kernel.shape[1])


def conv_same_weight(images, grads, side):
    padded = padded_grid(images, side)
    flat = flatten_rows(grads)
    terms = []
    for row in range(3):
        for column in range(3):
            window = padded[:, row : row + side, column : column + side, :].reshape(
                -1, images.shape[2]
            )
            terms.append(
                lax.dot_general(
                    window, flat, (((0,), (0,)), ((), ())), preferred_element_type=jnp.float32
                )
            )
    return jnp.stack(terms)


def conv_half_back(grads, kernel, side):
    half = side // 2
    count = grads.shape[0]
    flat = flatten_rows(grads)
    canvas = None
    for row in range(3):
        for column in range(3):
            term = lax.dot_general(
                flat,
                kernel[3 * row + column],
                (((1,), (1,)), ((), ())),
                preferred_element_type=jnp.float32,
            )
            term = term.reshape(count, half, half, kernel.shape[1])
            placed = lax.pad(
                term,
                jnp.zeros((), term.dtype),
                ((0, 0, 0), (row, 3 - row, 1), (column, 3 - column, 1), (0, 0, 0)),
            )
            canvas = placed if canvas is None else canvas + placed
    return canvas[:, 1 : side + 1, 1 : side + 1, :].reshape(count, side * side, kernel.shape[1])


def conv_half_weight(images, grads, side):
    padded = padded_grid(images, side)
    flat = flatten_rows(grads)
    terms = []
    for row in range(3):
        for column in range(3):
            window = padded[:, row : row + side : 2, column : column + side : 2, :].reshape(
                -1, images.shape[2]
            )
            terms.append(
                lax.dot_general(
                    window, flat, (((0,), (0,)), ((), ())), preferred_element_type=jnp.float32
                )
            )
    return jnp.stack(terms)


def gather_outer(shard):
    return lax.all_gather(shard, "cout", axis=2, tiled=True)


def gather_inner(shard):
    return lax.all_gather(shard, "cin", axis=2, tiled=True)


def sum_inner(partial_value):
    return lax.psum_scatter(partial_value, "cin", scatter_dimension=2, tiled=True)


def sum_outer(partial_value):
    return lax.psum_scatter(partial_value, "cout", scatter_dimension=2, tiled=True)


def shards(
    inner_features,
    block_input,
    first_kernel,
    expand_weight,
    reduce_weight,
    stride_kernel,
    output_grad,
):
    feature_block = gather_outer(inner_features)
    first_hidden = sum_inner(conv_same(feature_block, first_kernel, SIDE))
    first_act = smooth_gate(first_hidden).astype(jnp.bfloat16)
    first_block = gather_inner(first_act)
    expanded = sum_outer(project(first_block, expand_weight))
    joined_pre = block_input.astype(jnp.float32) + expanded
    joined = smooth_gate(joined_pre).astype(jnp.bfloat16)
    joined_wide = gather_outer(joined)
    joined_pair = lax.all_to_all(joined_wide, "section", split_axis=2, concat_axis=0, tiled=True)
    hidden_part = project(joined_pair, reduce_weight)
    cotangent_block = gather_outer(output_grad)
    back_part = conv_half_back(cotangent_block, stride_kernel, SIDE)
    hidden_whole = lax.psum(hidden_part, ("section", "cin"))
    second_act = smooth_gate(hidden_whole).astype(jnp.bfloat16)
    back_whole = lax.psum(back_part, ("section", "cin"))
    masked_second = (back_whole * gate_slope(hidden_whole)).astype(jnp.bfloat16)
    stride_gradient = conv_half_weight(second_act, cotangent_block, SIDE)
    reduce_gradient = outer_rows(joined_pair, masked_second)
    joined_back = project_back(masked_second, reduce_weight)
    joined_home = lax.all_to_all(joined_back, "section", split_axis=0, concat_axis=2, tiled=True)
    back_joined = sum_outer(joined_home)
    input_gradient = (back_joined * gate_slope(joined_pre)).astype(jnp.bfloat16)
    input_wide = gather_outer(input_gradient)
    expand_local = outer_rows(first_block, input_wide)
    back_first = sum_inner(project_back(input_wide, expand_weight))
    masked_first = (back_first * gate_slope(first_hidden)).astype(jnp.bfloat16)
    masked_block = gather_inner(masked_first)
    inner_gradient = sum_outer(conv_same_back(masked_block, first_kernel, SIDE))
    first_local = conv_same_weight(feature_block, masked_block, SIDE)
    first_gradient, expand_gradient = (
        lax.psum(first_local.astype(jnp.bfloat16), "section").astype(jnp.float32),
        lax.psum(expand_local.astype(jnp.bfloat16), "section").astype(jnp.float32),
    )
    return (
        inner_gradient,
        input_gradient,
        first_gradient,
        expand_gradient,
        reduce_gradient,
        stride_gradient,
    )


def solution(mesh):
    return jax.shard_map(
        shards,
        mesh=mesh,
        in_specs=(
            P("section", None, ("cin", "cout")),
            P("section", None, ("cin", "cout")),
            P(None, "cin", "cout"),
            P("cout", "cin"),
            P(("cin", "section"), "cout"),
            P(None, "cout", ("section", "cin")),
            P(None, None, ("section", "cin", "cout")),
        ),
        out_specs=(
            P("section", None, ("cin", "cout")),
            P("section", None, ("cin", "cout")),
            P(None, "cin", "cout"),
            P("cout", "cin"),
            P(("cin", "section"), "cout"),
            P(None, "cout", ("section", "cin")),
        ),
        check_vma=False,
    )
```

profile of v0, /device:TPU:0, one launch (start us, length us, event | category | flops | bytes accessed | tf_op | source)
XLA Modules:
  0.0 957.9 jit_solution(9622084547646178098)
XLA Ops:
  7.2 30.3 %all_gather.19 = bf16[1,784,320]{1,2,0:T(8,128)(2,1)S(1)} all-gather(bf16[1,784,40]{1,2,0:T(8,128)(2,1)} %param.7), channel_id=1, replica_groups=mesh['section'=2,'cin'=8,'cout'=8] {'cout'}, dimensions={2}, use_global_device_ids=true | all-gather | bytes 564480 | tf_op jit(solution)/shard_map/all_gather | solution.py:137
  38.1 2.9 pad_slice_fusion.8
  42.1 2.3 reshape.187
  44.4 2.2 reshape.188
  46.5 2.1 reshape.189
  54.1 2.1 reshape.191
  56.2 2.1 reshape.192
  58.4 2.1 reshape.193
  60.5 2.1 reshape.194
  62.6 2.0 convolution_add_fusion.7
  68.5 28.8 %all_gather.18 = bf16[2,196,320]{1,2,0:T(8,128)(2,1)S(1)} all-gather(bf16[2,196,40]{1,2,0:T(8,128)(2,1)S(1)} %copy-done.55), channel_id=1, replica_groups=mesh['section'=2,'cin'=8,'cout'=8] {'cout'}, dimensions={2}, use_global_device_ids=true | all-gather | bytes 282240 | tf_op jit(solution)/shard_map/all_gather | solution.py:137
  98.0 2.5 fusion.54
  102.0 16.4 %pad.56 = f32[2,28,28,640]{3,2,1,0:T(8,128)} pad(f32[2,14,14,640]{3,2,1,0:T(8,128)} %fusion.54, f32[]{:T(128)} %constant.3.clone.1), padding=0_0_0x1_0_1x1_0_1x0_0_0 | pad | bytes 5017604 | tf_op jit(solution)/shard_map/slice | solution.py:116
  118.4 11.1 %pad.55 = f32[2,28,28,640]{3,2,1,0:T(8,128)} pad(f32[2,14,14,640]{3,2,1,0:T(8,128)S(1)} %fusion.56, f32[]{:T(128)} %constant.3.clone.1), padding=0_0_0x1_0_1x0_1_1x0_0_0 | pad | bytes 5017604 | tf_op jit(solution)/shard_map/slice | solution.py:116
  131.0 11.1 %pad.53 = f32[2,28,28,640]{3,2,1,0:T(8,128)} pad(f32[2,14,14,640]{3,2,1,0:T(8,128)S(1)} %fusion.60, f32[]{:T(128)} %constant.3.clone.1), padding=0_0_0x0_1_1x1_0_1x0_0_0 | pad | bytes 5017604 | tf_op jit(solution)/shard_map/slice | solution.py:116
  143.6 11.1 %pad.52 = f32[2,28,28,640]{3,2,1,0:T(8,128)} pad(f32[2,14,14,640]{3,2,1,0:T(8,128)S(1)} %fusion.62, f32[]{:T(128)} %constant.3.clone.1), padding=0_0_0x0_1_1x0_1_1x0_0_0 | pad | bytes 5017604 | tf_op jit(solution)/shard_map/slice | solution.py:116
  156.2 11.3 %pad.41 = f32[2,30,30,640]{3,2,1,0:T(8,128)} pad(f32[2,14,14,640]{3,2,1,0:T(8,128)S(1)} %fusion.66, f32[]{:T(128)} %constant.3.clone.1), padding=0_0_0x0_3_1x2_1_1x0_0_0 | pad | bytes 5611524 | tf_op jit(solution)/shard_map/pad | solution.py:110
  168.9 11.2 %pad.39 = f32[2,30,30,640]{3,2,1,0:T(8,128)} pad(f32[2,14,14,640]{3,2,1,0:T(8,128)S(1)} %fusion.70, f32[]{:T(128)} %constant.3.clone.1), padding=0_0_0x0_3_1x0_3_1x0_0_0 | pad | bytes 5611524 | tf_op jit(solution)/shard_map/pad | solution.py:110
  181.6 11.3 %pad.40 = f32[2,30,30,640]{3,2,1,0:T(8,128)} pad(f32[2,14,14,640]{3,2,1,0:T(8,128)S(1)} %fusion.68, f32[]{:T(128)} %constant.3.clone.1), padding=0_0_0x0_3_1x1_2_1x0_0_0 | pad | bytes 5611524 | tf_op jit(solution)/shard_map/pad | solution.py:110
  194.4 11.1 %pad.74 = f32[2,28,29,640]{3,2,1,0:T(8,128)} pad(f32[2,14,14,640]{3,2,1,0:T(8,128)S(1)} %fusion.64, f32[]{:T(128)} %constant.3.clone.1), padding=0_0_0x0_1_1x0_2_1x0_0_0 | pad | bytes 5160964
  207.0 11.2 %pad.73 = f32[2,28,29,640]{3,2,1,0:T(8,128)} pad(f32[2,14,14,640]{3,2,1,0:T(8,128)S(1)} %fusion.58, f32[]{:T(128)} %constant.3.clone.1), padding=0_0_0x1_0_1x0_2_1x0_0_0 | pad | bytes 5160964
  219.1 36.6 %all_gather.20 = bf16[1,784,320]{1,2,0:T(8,128)(2,1)S(1)} all-gather(bf16[1,784,40]{1,2,0:T(8,128)(2,1)S(1)} %multiply_convert_fusion.4), channel_id=1, replica_groups=mesh['section'=2,'cin'=8,'cout'=8] {'cin'}, dimensions={2}, use_global_device_ids=true | all-gather | bytes 564480 | tf_op jit(solution)/shard_map/all_gather | solution.py:141
  257.3 4.1 copy.97
  261.8 6.8 add_add_fusion
  268.6 11.1 %fusion.4 = f32[2,28,28,640]{3,2,1,0:T(8,128)S(1)} fusion(f32[2,28,28,640]{3,2,1,0:T(8,128)} %pad.56, f32[2,28,28,640]{3,2,1,0:T(8,128)} %pad.55, f32[2,28,28,640]{3,2,1,0:T(8,128)} %pad.53, f32[2,28,28,640]{3,2,1,0:T(8,128)} %pad.52, f32[2,30,30,640]{3,2,1,0:T(8,128)S(1)} %add_add_fusion, f32[2,28,29,640]{3,2,1,0:T(8,128)} %pad.74, f32[2,28,29,640]{3,2,1,0:T(8,128)} %pad.73), kind=kLoop, calls=%fused_computation.6 | loop fusion | flops 6021120 | bytes 32112640 | tf_op jit(solution)/shard_map/add | solution.py:115
  279.7 3.1 copy.94
  282.8 2.2 copy.95
  286.3 58.8 %all-reduce.24.cloned.1.call-done = f32[1,784,640]{1,0,2:T(1,128)} async-done(((f32[1,784,640]{1,0,2:T(1,128)}), f32[1,784,640]{1,0,2:T(1,128)}) %all-reduce.24.cloned.1.call-update) | async-done | bytes 2007056
  346.9 31.0 %all_gather.21 = bf16[1,784,640]{1,2,0:T(8,128)(2,1)S(1)} all-gather(bf16[1,784,80]{1,2,0:T(8,128)(2,1)S(1)} %multiply_convert_fusion.2), channel_id=1, replica_groups=mesh['section'=2,'cin'=8,'cout'=8] {'cout'}, dimensions={2}, use_global_device_ids=true | all-gather | bytes 1128960 | tf_op jit(solution)/shard_map/all_gather | solution.py:137
  380.2 9.0 reduce
  389.1 3.1 reshape.245
  392.2 4.7 all_to_all.33
  396.9 2.6 reshape.246
  399.5 1.8 copy.132
  401.3 3.3 fusion.74
  404.7 195.4 %all-reduce.28.cloned.1.call-done = (f32[2,784,640]{2,1,0:T(8,128)}, f32[2,784,640]{2,1,0:T(8,128)}) async-done(((f32[2,784,640]{2,1,0:T(8,128)}, f32[2,784,640]{2,1,0:T(8,128)}), (f32[2,784,640]{2,1,0:T(8,128)}, f32[2,784,640]{2,1,0:T(8,128)})) %all-reduce.28.cloned.1.call-update) | async-done | bytes 8028176 | tf_op jit(solution)/shard_map/psum | solution.py:175
  600.2 5.1 multiply_convert_fusion
  606.6 5.6 all_to_all.34
  612.2 3.7 copy.100
  616.0 83.4 %all-reduce.26.cloned.1.call-done = f32[1,784,640]{1,0,2:T(1,128)} async-done(((f32[1,784,640]{1,0,2:T(1,128)}), f32[1,784,640]{1,0,2:T(1,128)}) %all-reduce.26.cloned.1.call-update) | async-done | bytes 2007056
  700.6 30.6 %all_gather.22 = bf16[1,784,640]{1,2,0:T(8,128)(2,1)S(1)} all-gather(bf16[1,784,80]{1,2,0:T(8,128)(2,1)S(1)} %fusion.85), channel_id=1, replica_groups=mesh['section'=2,'cin'=8,'cout'=8] {'cout'}, dimensions={2}, use_global_device_ids=true | all-gather | bytes 1128960 | tf_op jit(solution)/shard_map/all_gather | solution.py:137
  734.5 2.2 copy.104
  736.7 3.6 reshape.211
  741.9 5.0 fusion.137
  749.9 2.5 fusion.19
  752.3 2.4 fusion.18
  756.3 45.9 %reduce-scatter.16.cloned.1.call-done = f32[1,784,40]{1,2,0:T(8,128)} async-done(((f32[1,784,320]{1,2,0:T(8,128)}), f32[1,784,40]{1,2,0:T(8,128)}) %reduce-scatter.16.cloned.1.call-update) | async-done | bytes 125456
  803.2 35.5 %all_gather.23 = bf16[1,784,320]{1,2,0:T(8,128)(2,1)S(1)} all-gather(bf16[1,784,40]{1,2,0:T(8,128)(2,1)S(1)} %multiply_convert_fusion.3), channel_id=1, replica_groups=mesh['section'=2,'cin'=8,'cout'=8] {'cin'}, dimensions={2}, use_global_device_ids=true | all-gather | bytes 564480 | tf_op jit(solution)/shard_map/all_gather | solution.py:141
  841.3 6.5 pad_slice_fusion.4
  847.9 2.1 reshape.209
  850.0 2.6 fusion.86
  852.6 2.1 reshape.208
  854.7 2.2 reshape.207
  856.9 2.2 reshape.206
  859.1 2.1 reshape.201
  861.3 2.1 reshape.202
  863.4 2.1 reshape.203
  865.5 2.1 reshape.204
  867.7 2.6 fusion.23
  870.3 2.6 fusion.25
  902.4 2.0 fusion.138
  904.3 2.3 all-reduce.30.cloned.1.call-done
  906.7 4.1 convert_element_type.43
  911.7 38.9 %reduce-scatter.18.cloned.1.call-done = f32[1,784,40]{1,2,0:T(8,128)} async-done(((f32[1,784,320]{1,2,0:T(8,128)}), f32[1,784,40]{1,2,0:T(8,128)}) %reduce-scatter.18.cloned.1.call-update) | async-done | bytes 125456
  (208 shorter events, 76.6 us)
Async XLA Ops:
  7.2 394.1 %copy-start = (bf16[320,640]{1,0:T(8,128)(2,1)S(1)}, bf16[320,640]{1,0:T(8,128)(2,1)}, u32[]{:S(2)}) copy-start(bf16[320,640]{1,0:T(8,128)(2,1)} %param.11) | copy-start | bytes 1228804
  7.2 211.0 %reduce-scatter.14.cloned.1.call-start = ((), (), s32[]{:S(2)}) async-start(), calls=%async_computation.7 | async-start | bytes 1290240
  42.1 6.6 copy-start.1
  48.7 1.7 copy-start.19
  48.7 2.3 copy-start.18
  50.9 1.1 copy-start.16
  62.6 2.0 copy-start.24
  64.7 1.1 copy-start.20
  65.8 1.1 copy-start.22
  66.8 1.6 copy-start.55
  68.4 276.6 %all-reduce.24.cloned.1.call-start = ((), (), s32[]{:S(2)}) async-start(), calls=%async_computation.5 | async-start | bytes 4587520
  97.3 0.7 copy-start.12
  206.9 49.6 %copy-start.48 = (bf16[320,640]{1,0:T(8,128)(2,1)S(1)}, bf16[320,640]{1,0:T(8,128)(2,1)}, u32[]{:S(2)}) copy-start(bf16[320,640]{1,0:T(8,128)(2,1)} %param.10) | copy-start | bytes 1228804
  255.7 0.8 copy-start.35
  261.5 338.7 %all-reduce.28.cloned.1.call-start = ((), (), s32[]{:S(2)}) async-start(), calls=%async_computation.10 | async-start | bytes 16056320 | tf_op jit(solution)/shard_map/psum | solution.py:175
  282.8 2.2 copy-start.56
  282.8 63.3 %copy-start.52 = (bf16[1,784,80]{1,2,0:T(8,128)(2,1)S(1)}, bf16[1,784,80]{1,2,0:T(8,128)(2,1)}, u32[]{:S(2)}) copy-start(bf16[1,784,80]{1,2,0:T(8,128)(2,1)} %param.8) | copy-start | bytes 376324
  346.1 0.7 copy-start.14
  404.7 294.7 %all-reduce.26.cloned.1.call-start = ((), (), s32[]{:S(2)}) async-start(), calls=%async_computation.6 | async-start | bytes 4587520
  605.3 1.3 copy-start.3
  615.9 84.6 %copy-start.15 = (f32[1,784,80]{1,0,2:T(1,128)S(1)}, f32[1,784,80]{1,0,2:T(1,128)}, u32[]{:S(2)}) copy-start(f32[1,784,80]{1,0,2:T(1,128)} %copy-done.14) | copy-start | bytes 752644
  615.9 116.3 %copy-start.49 = (bf16[320,640]{1,0:T(8,128)(2,1)S(1)}, bf16[320,640]{1,0:T(8,128)(2,1)}, u32[]{:S(2)}) copy-start(bf16[320,640]{1,0:T(8,128)(2,1)} %param.10) | copy-start | bytes 1228804
  615.9 186.3 %reduce-scatter.16.cloned.1.call-start = ((), (), s32[]{:S(2)}) async-start(), calls=%async_computation.8 | async-start | bytes 1290240
  700.6 33.3 %copy-start.51 = (bf16[1,784,80]{1,2,0:T(8,128)(2,1)}, bf16[1,784,80]{1,2,0:T(8,128)(2,1)S(1)}, u32[]{:S(2)}) copy-start(bf16[1,784,80]{1,2,0:T(8,128)(2,1)S(1)} %fusion.85) | copy-start | bytes 376324
  731.2 1.0 copy-start.9
  732.2 2.0 copy-start.13
  733.9 172.8 %all-reduce.30.cloned.1.call-start = ((), (), s32[]{:S(2)}) async-start(), calls=%async_computation.11 | async-start | bytes 5242880 | tf_op jit(solution)/shard_map/psum | solution.py:191
  736.7 3.6 copy-start.5
  748.9 5.8 copy-start.10
  749.9 4.9 copy-start.36
  752.3 49.9 %copy-start.53 = (f32[1,784,40]{1,2,0:T(8,128)S(1)}, f32[1,784,40]{1,2,0:T(8,128)}, u32[]{:S(2)}) copy-start(f32[1,784,40]{1,2,0:T(8,128)} %reduce-scatter.14.cloned.1.call-done) | copy-start | bytes 376324
  754.8 84.3 %copy-start.27 = (bf16[784,320]{1,0:T(8,128)(2,1)S(1)}, bf16[784,320]{1,0:T(8,128)(2,1)}, u32[]{:S(2)}) copy-start(bf16[784,320]{1,0:T(8,128)(2,1)} %reshape.186) | copy-start | bytes 1505284
  838.7 1.6 copy-start.6
  841.3 8.6 copy-start.2
  867.7 5.2 copy-start.7
  867.7 5.2 copy-start.17
  870.3 5.0 copy-start.26
  872.9 3.7 copy-start.25
  874.1 3.7 copy-start.21
  875.3 3.8 copy-start.23
  879.1 1.6 copy-start.30
  880.4 70.2 %reduce-scatter.18.cloned.1.call-start = ((), (), s32[]{:S(2)}) async-start(), calls=%async_computation.9 | async-start | bytes 1290240
  880.8 1.1 copy-start.31
  880.8 1.6 copy-start.32
  881.9 1.1 copy-start.33
  882.4 1.1 copy-start.34
  883.0 1.1 copy-start.28
  884.1 1.1 copy-start.29
  885.2 1.1 copy-start.8
  885.2 1.4 copy-start.11
  886.6 1.6 copy-start.43
  888.2 1.4 copy-start.42
  888.2 1.6 copy-start.41
  889.6 1.3 copy-start.40
  889.8 2.0 copy-start.39
  890.9 1.2 copy-start.38
  891.9 1.3 copy-start.37
  892.2 3.4 copy-start.44
  893.2 3.7 copy-start.45
  895.6 4.1 copy-start.46
  896.9 4.1 copy-start.47
  898.3 4.1 copy-start.4
  898.3 4.1 copy-start.50
  906.7 4.1 copy-start.54
Sparse Core Ops, SparseCore 0:
  68.6 69.3 reduce-scatter.13
  261.6 83.4 all-reduce.23
  404.8 195.3 all-reduce.27
  616.1 83.3 all-reduce.25
  734.0 68.1 reduce-scatter.15
  880.6 26.0 all-reduce.29
  909.6 40.9 reduce-scatter.17
where the time goes:
time: 967 us; the launch traced here: 958 us
  waiting for transfers between devices  425 us (44%)
  local copies, waits for them, and re-layouts  203 us (21%)
  blocking collectives  203 us (21%)
  matrix products  70.4 us (7%)
  other arithmetic  39.2 us (4%)
  between operations  15.9 us (2%)
    unnamed x12, waiting for transfers between devices  227 us
    psum x1, waiting for transfers between devices, shards(): back_whole = lax.psum(back_part, ('section', 'cin'))  195 us
    all_gather x4, blocking collectives, gather_outer(): return lax.all_gather(shard, 'cout', axis=2, tiled=True)  121 us
    all_gather x2, blocking collectives, gather_inner(): return lax.all_gather(shard, 'cin', axis=2, tiled=True)  72.1 us
    slice x5, local copies, waits for them, and re-layouts, conv_half_back(): canvas[:, 1:side + 1, 1:side + 1, :]  52.9 us
    unnamed x123, local copies, waits for them, and re-layouts  39.9 us
    pad x3, local copies, waits for them, and re-layouts, conv_half_back(): lax.pad(term, jnp.zeros((), term.dtype), ((0, 0, 0), (row, 3 - row, 1), (...  33.8 us
  transfers between devices with their start and end apart: 7, of which 6 were waited for; matrix products, arithmetic and copies ran while one was open for 20% of the time, Pallas kernels for 0%

commit v1 on v0

--- a/solution.py
+++ b/solution.py
@@ -172,7 +172,7 @@
     back_part = conv_half_back(cotangent_block, stride_kernel, SIDE)
     hidden_whole = lax.psum(hidden_part, ("section", "cin"))
     second_act = smooth_gate(hidden_whole).astype(jnp.bfloat16)
-    back_whole = lax.psum(back_part, ("section", "cin"))
+    back_whole = lax.psum(lax.psum(back_part, "cin"), "section")
     masked_second = (back_whole * gate_slope(hidden_whole)).astype(jnp.bfloat16)
     stride_gradient = conv_half_weight(second_act, cotangent_block, SIDE)
     reduce_gradient = outer_rows(joined_pair, masked_second)

time: 967 us -> 1070 us (1.11)
  waiting for transfers between devices: 425 us -> 487 us
  local copies, waits for them, and re-layouts: 203 us -> 235 us
    psum x1 -> x3, waiting for transfers between devices: 195 us -> 229 us  [the longest x1 164 us: shards(): hidden_whole = lax.psum(hidden_part, ('section', 'cin'))]
    unnamed x12 -> x14, waiting for transfers between devices: 227 us -> 255 us
    slice x5, local copies, waits for them, and re-layouts: 52.9 us -> 68.5 us  [conv_half_back(): canvas[:, 1:side + 1, 1:side + 1, :]]
    unnamed x123 -> x115, local copies, waits for them, and re-layouts: 39.9 us -> 51.6 us
  transfers between devices with their start and end apart: 7 -> 9, of which waited for: 6 -> 7; matrix products, arithmetic and copies ran while one was open for 20% -> 25% of each run, Pallas kernels for 0% -> 0%
where the time goes in v1:
time: 1070 us; the launch traced here: 1050 us
  waiting for transfers between devices  487 us (46%)
  local copies, waits for them, and re-layouts  235 us (22%)
  blocking collectives  205 us (19%)
  matrix products  71.1 us (7%)
  other arithmetic  38.7 us (4%)
  between operations  15.7 us (1%)
    unnamed x14, waiting for transfers between devices  255 us
    psum x1, waiting for transfers between devices, shards(): hidden_whole = lax.psum(hidden_part, ('section', 'cin'))  164 us
    all_gather x4, blocking collectives, gather_outer(): return lax.all_gather(shard, 'cout', axis=2, tiled=True)  120 us
    all_gather x2, blocking collectives, gather_inner(): return lax.all_gather(shard, 'cin', axis=2, tiled=True)  74.1 us
    slice x5, local copies, waits for them, and re-layouts, conv_half_back(): canvas[:, 1:side + 1, 1:side + 1, :]  68.5 us
    psum x2, waiting for transfers between devices, shards(): back_whole = lax.psum(lax.psum(back_part, 'cin'), 'section')  64.6 us
    unnamed x115, local copies, waits for them, and re-layouts  51.6 us
    pad x3, local copies, waits for them, and re-layouts, conv_half_back(): lax.pad(term, jnp.zeros((), term.dtype), ((0, 0, 0), (row, 3 - row, 1), (...  44.3 us
  transfers between devices with their start and end apart: 9, of which 7 were waited for; matrix products, arithmetic and copies ran while one was open for 25% of the time, Pallas kernels for 0%

profile of v1, /device:TPU:0, one launch (start us, length us, event | category | flops | bytes accessed | tf_op | source)
XLA Modules:
  0.0 1053.3 jit_solution(2674147945746028612)
XLA Ops:
  7.2 30.3 %all_gather.19 = bf16[1,784,320]{1,2,0:T(8,128)(2,1)S(1)} all-gather(bf16[1,784,40]{1,2,0:T(8,128)(2,1)} %param.7), channel_id=1, replica_groups=mesh['section'=2,'cin'=8,'cout'=8] {'cout'}, dimensions={2}, use_global_device_ids=true | all-gather | bytes 564480 | tf_op jit(solution)/shard_map/all_gather | solution.py:137
  38.9 6.2 pad_slice_fusion.8
  45.1 2.1 reshape.194
  47.2 2.1 reshape.187
  52.6 2.3 reshape.192
  54.9 2.1 reshape.193
  57.1 2.1 reshape.186
  69.0 28.8 %all_gather.18 = bf16[2,196,320]{1,2,0:T(8,128)(2,1)S(1)} all-gather(bf16[2,196,40]{1,2,0:T(8,128)(2,1)S(1)} %copy-done.49), channel_id=1, replica_groups=mesh['section'=2,'cin'=8,'cout'=8] {'cout'}, dimensions={2}, use_global_device_ids=true | all-gather | bytes 282240 | tf_op jit(solution)/shard_map/all_gather | solution.py:137
  100.2 2.5 fusion.66
  113.2 16.4 %pad.56 = f32[2,28,28,640]{3,2,1,0:T(8,128)} pad(f32[2,14,14,640]{3,2,1,0:T(8,128)} %fusion.54, f32[]{:T(128)} %constant.3.clone.1), padding=0_0_0x1_0_1x1_0_1x0_0_0 | pad | bytes 5017604 | tf_op jit(solution)/shard_map/slice | solution.py:116
  129.7 16.3 %pad.55 = f32[2,28,28,640]{3,2,1,0:T(8,128)} pad(f32[2,14,14,640]{3,2,1,0:T(8,128)} %fusion.56, f32[]{:T(128)} %constant.3.clone.1), padding=0_0_0x1_0_1x0_1_1x0_0_0 | pad | bytes 5017604 | tf_op jit(solution)/shard_map/slice | solution.py:116
  146.0 16.3 %pad.73 = f32[2,28,29,640]{3,2,1,0:T(8,128)} pad(f32[2,14,14,640]{3,2,1,0:T(8,128)} %fusion.58, f32[]{:T(128)} %constant.3.clone.1), padding=0_0_0x1_0_1x0_2_1x0_0_0 | pad | bytes 5160964
  162.3 16.3 %pad.53 = f32[2,28,28,640]{3,2,1,0:T(8,128)} pad(f32[2,14,14,640]{3,2,1,0:T(8,128)} %fusion.60, f32[]{:T(128)} %constant.3.clone.1), padding=0_0_0x0_1_1x1_0_1x0_0_0 | pad | bytes 5017604 | tf_op jit(solution)/shard_map/slice | solution.py:116
  178.7 16.3 %pad.52 = f32[2,28,28,640]{3,2,1,0:T(8,128)} pad(f32[2,14,14,640]{3,2,1,0:T(8,128)} %fusion.62, f32[]{:T(128)} %constant.3.clone.1), padding=0_0_0x0_1_1x0_1_1x0_0_0 | pad | bytes 5017604 | tf_op jit(solution)/shard_map/slice | solution.py:116
  194.9 16.4 %pad.74 = f32[2,28,29,640]{3,2,1,0:T(8,128)} pad(f32[2,14,14,640]{3,2,1,0:T(8,128)} %fusion.64, f32[]{:T(128)} %constant.3.clone.1), padding=0_0_0x0_1_1x0_2_1x0_0_0 | pad | bytes 5160964
  211.3 16.5 %pad.39 = f32[2,30,30,640]{3,2,1,0:T(8,128)} pad(f32[2,14,14,640]{3,2,1,0:T(8,128)} %fusion.70, f32[]{:T(128)} %constant.3.clone.1), padding=0_0_0x0_3_1x0_3_1x0_0_0 | pad | bytes 5611524 | tf_op jit(solution)/shard_map/pad | solution.py:110
  227.8 16.5 %pad.41 = f32[2,30,30,640]{3,2,1,0:T(8,128)} pad(f32[2,14,14,640]{3,2,1,0:T(8,128)} %fusion.66, f32[]{:T(128)} %constant.3.clone.1), padding=0_0_0x0_3_1x2_1_1x0_0_0 | pad | bytes 5611524 | tf_op jit(solution)/shard_map/pad | solution.py:110
  244.3 11.3 %pad.40 = f32[2,30,30,640]{3,2,1,0:T(8,128)} pad(f32[2,14,14,640]{3,2,1,0:T(8,128)S(1)} %fusion.68, f32[]{:T(128)} %constant.3.clone.1), padding=0_0_0x0_3_1x1_2_1x0_0_0 | pad | bytes 5611524 | tf_op jit(solution)/shard_map/pad | solution.py:110
  255.6 6.9 add_add_fusion
  262.6 9.5 fusion.4
  272.1 3.1 copy.94
  275.2 2.2 copy.95
  278.5 38.6 %all_gather.20 = bf16[1,784,320]{1,2,0:T(8,128)(2,1)S(1)} all-gather(bf16[1,784,40]{1,2,0:T(8,128)(2,1)S(1)} %multiply_convert_fusion.4), channel_id=1, replica_groups=mesh['section'=2,'cin'=8,'cout'=8] {'cin'}, dimensions={2}, use_global_device_ids=true | all-gather | bytes 564480 | tf_op jit(solution)/shard_map/all_gather | solution.py:141
  317.9 1.8 convolution_bitcast_fusion
  319.8 3.8 copy.97
  323.6 64.6 %all-reduce.25.cloned.1.call-done = f32[2,784,640]{2,1,0:T(8,128)} async-done(((f32[2,784,640]{2,1,0:T(8,128)}), f32[2,784,640]{2,1,0:T(8,128)}) %all-reduce.25.cloned.1.call-update) | async-done | bytes 4014096 | tf_op jit(solution)/shard_map/psum | solution.py:175
  389.5 85.1 %all-reduce.31.cloned.1.call-done = f32[1,784,640]{1,0,2:T(1,128)} async-done(((f32[1,784,640]{1,0,2:T(1,128)}), f32[1,784,640]{1,0,2:T(1,128)}) %all-reduce.31.cloned.1.call-update) | async-done | bytes 2007056
  476.4 30.5 %all_gather.21 = bf16[1,784,640]{1,2,0:T(8,128)(2,1)S(1)} all-gather(bf16[1,784,80]{1,2,0:T(8,128)(2,1)S(1)} %multiply_convert_fusion.2), channel_id=1, replica_groups=mesh['section'=2,'cin'=8,'cout'=8] {'cout'}, dimensions={2}, use_global_device_ids=true | all-gather | bytes 1128960 | tf_op jit(solution)/shard_map/all_gather | solution.py:137
  509.2 9.0 reduce
  518.2 3.1 reshape.245
  521.2 4.7 all_to_all.33
  525.9 2.6 reshape.246
  528.6 1.8 copy.132
  530.4 3.3 fusion.74
  533.8 164.5 %all-reduce.29.cloned.1.call-done = f32[2,784,640]{2,1,0:T(8,128)} async-done(((f32[2,784,640]{2,1,0:T(8,128)}), f32[2,784,640]{2,1,0:T(8,128)}) %all-reduce.29.cloned.1.call-update) | async-done | bytes 4014096 | tf_op jit(solution)/shard_map/psum | solution.py:173
  698.3 5.1 multiply_convert_fusion
  704.8 5.6 all_to_all.34
  710.3 3.7 copy.100
  714.1 86.0 %all-reduce.33.cloned.1.call-done = f32[1,784,640]{1,0,2:T(1,128)} async-done(((f32[1,784,640]{1,0,2:T(1,128)}), f32[1,784,640]{1,0,2:T(1,128)}) %all-reduce.33.cloned.1.call-update) | async-done | bytes 2007056
  802.0 30.5 %all_gather.22 = bf16[1,784,640]{1,2,0:T(8,128)(2,1)S(1)} all-gather(bf16[1,784,80]{1,2,0:T(8,128)(2,1)S(1)} %fusion.85), channel_id=1, replica_groups=mesh['section'=2,'cin'=8,'cout'=8] {'cout'}, dimensions={2}, use_global_device_ids=true | all-gather | bytes 1128960 | tf_op jit(solution)/shard_map/all_gather | solution.py:137
  835.9 2.2 copy.104
  838.1 3.6 reshape.211
  843.3 5.0 fusion.137
  851.3 2.5 fusion.19
  853.8 2.4 fusion.18
  857.7 45.9 %reduce-scatter.16.cloned.1.call-done = f32[1,784,40]{1,2,0:T(8,128)} async-done(((f32[1,784,320]{1,2,0:T(8,128)}), f32[1,784,40]{1,2,0:T(8,128)}) %reduce-scatter.16.cloned.1.call-update) | async-done | bytes 125456
  904.6 35.5 %all_gather.23 = bf16[1,784,320]{1,2,0:T(8,128)(2,1)S(1)} all-gather(bf16[1,784,40]{1,2,0:T(8,128)(2,1)S(1)} %multiply_convert_fusion.3), channel_id=1, replica_groups=mesh['section'=2,'cin'=8,'cout'=8] {'cin'}, dimensions={2}, use_global_device_ids=true | all-gather | bytes 564480 | tf_op jit(solution)/shard_map/all_gather | solution.py:141
  940.5 2.3 fusion.21
  943.0 2.4 fusion.23
  945.3 2.4 fusion.25
  955.3 2.7 pad_slice_fusion.4
  958.2 2.4 reshape.202
  960.6 2.2 reshape.203
  962.8 2.1 reshape.206
  964.9 2.6 fusion.95
  967.5 2.1 reshape.207
  969.7 2.1 reshape.208
  971.8 2.1 reshape.209
  973.9 2.1 reshape.201
  997.0 2.0 fusion.138
  999.0 3.4 all-reduce.35.cloned.1.call-done
  1002.3 1.9 convert_element_type.45
  1004.3 4.1 convert_element_type.43
  1008.3 37.9 %reduce-scatter.18.cloned.1.call-done = f32[1,784,40]{1,2,0:T(8,128)} async-done(((f32[1,784,320]{1,2,0:T(8,128)}), f32[1,784,40]{1,2,0:T(8,128)}) %reduce-scatter.18.cloned.1.call-update) | async-done | bytes 125456
  (207 shorter events, 76.6 us)
Async XLA Ops:
  7.2 523.2 %copy-start = (bf16[320,640]{1,0:T(8,128)(2,1)S(1)}, bf16[320,640]{1,0:T(8,128)(2,1)}, u32[]{:S(2)}) copy-start(bf16[320,640]{1,0:T(8,128)(2,1)} %param.11) | copy-start | bytes 1228804
  7.2 270.3 %reduce-scatter.14.cloned.1.call-start = ((), (), s32[]{:S(2)}) async-start(), calls=%async_computation.10 | async-start | bytes 1290240
  52.6 6.6 copy-start.1
  59.2 1.7 copy-start.27
  59.2 2.3 copy-start.26
  61.5 1.1 copy-start.24
  63.1 1.1 copy-start.22
  64.1 1.1 copy-start.20
  65.2 1.1 copy-start.18
  66.3 1.1 copy-start.16
  67.4 1.6 copy-start.49
  68.9 319.3 %all-reduce.25.cloned.1.call-start = ((), (), s32[]{:S(2)}) async-start(), calls=%async_computation.5 | async-start | bytes 8028160 | tf_op jit(solution)/shard_map/psum | solution.py:175
  97.8 0.7 copy-start.12
  98.5 4.1 copy-start.11
  244.3 18.2 %slice-start = ((s8[4587520]{0:T(1024)(128)(4,1)}), s8[393216]{0:T(1024)(128)(4,1)S(1)}, s32[]{:S(2)}) async-start(s8[4587520]{0:T(1024)(128)(4,1)} %bitcast.323), calls=%async_computation.14 | async-start | bytes 786432
  255.6 7.0 slice-start.1
  277.4 197.2 %all-reduce.31.cloned.1.call-start = ((), (), s32[]{:S(2)}) async-start(), calls=%async_computation.8 | async-start | bytes 4587520
  317.1 0.9 copy-start.33
  323.6 64.7 %copy-start.50 = (u32[128]{0:T(128)S(1)}, u32[128]{0:T(128)}, u32[]{:S(2)}) copy-start(u32[128]{0:T(128)} %constant.42) | copy-start | bytes 1540
  323.6 210.2 %all-reduce.27.cloned.1.call-start = ((), (), s32[]{:S(2)}) async-start(), calls=%async_computation.6 | async-start | bytes 8028160 | tf_op jit(solution)/shard_map/psum | solution.py:175
  388.2 87.5 %copy-start.47 = (bf16[1,784,80]{1,2,0:T(8,128)(2,1)S(1)}, bf16[1,784,80]{1,2,0:T(8,128)(2,1)}, u32[]{:S(2)}) copy-start(bf16[1,784,80]{1,2,0:T(8,128)(2,1)} %param.8) | copy-start | bytes 376324
  388.2 310.1 %all-reduce.29.cloned.1.call-start = ((), (), s32[]{:S(2)}) async-start(), calls=%async_computation.7 | async-start | bytes 8028160 | tf_op jit(solution)/shard_map/psum | solution.py:173
  475.7 0.7 copy-start.14
  533.7 266.4 %all-reduce.33.cloned.1.call-start = ((), (), s32[]{:S(2)}) async-start(), calls=%async_computation.9 | async-start | bytes 4587520
  703.4 1.3 copy-start.3
  714.1 87.1 %copy-start.15 = (f32[1,784,80]{1,0,2:T(1,128)S(1)}, f32[1,784,80]{1,0,2:T(1,128)}, u32[]{:S(2)}) copy-start(f32[1,784,80]{1,0,2:T(1,128)} %copy-done.14) | copy-start | bytes 752644
  714.1 119.6 %copy-start.44 = (bf16[320,640]{1,0:T(8,128)(2,1)S(1)}, bf16[320,640]{1,0:T(8,128)(2,1)}, u32[]{:S(2)}) copy-start(bf16[320,640]{1,0:T(8,128)(2,1)} %param.10) | copy-start | bytes 1228804
  714.1 189.5 %reduce-scatter.16.cloned.1.call-start = ((), (), s32[]{:S(2)}) async-start(), calls=%async_computation.11 | async-start | bytes 1290240
  801.3 0.7 copy-start.46
  832.6 1.1 copy-start.8
  833.6 1.9 copy-start.13
  835.3 167.0 %all-reduce.35.cloned.1.call-start = ((), (), s32[]{:S(2)}) async-start(), calls=%async_computation.13 | async-start | bytes 5242880 | tf_op jit(solution)/shard_map/psum | solution.py:191
  838.1 3.7 copy-start.5
  850.3 5.9 copy-start.9
  851.3 4.9 copy-start.34
  853.8 49.8 %copy-start.48 = (f32[1,784,40]{1,2,0:T(8,128)S(1)}, f32[1,784,40]{1,2,0:T(8,128)}, u32[]{:S(2)}) copy-start(f32[1,784,40]{1,2,0:T(8,128)} %reduce-scatter.14.cloned.1.call-done) | copy-start | bytes 376324
  940.1 13.9 %copy-start.6 = (bf16[1,784,320]{1,2,0:T(8,128)(2,1)}, bf16[1,784,320]{1,2,0:T(8,128)(2,1)S(1)}, u32[]{:S(2)}) copy-start(bf16[1,784,320]{1,2,0:T(8,128)(2,1)S(1)} %all_gather.23) | copy-start | bytes 1505284
  942.9 4.8 copy-start.25
  945.3 4.9 copy-start.23
  947.7 3.7 copy-start.21
  949.0 3.7 copy-start.19
  950.2 3.8 copy-start.17
  958.2 6.7 copy-start.2
  976.0 70.2 %reduce-scatter.18.cloned.1.call-start = ((), (), s32[]{:S(2)}) async-start(), calls=%async_computation.12 | async-start | bytes 1290240
  976.4 1.7 copy-start.30
  976.4 2.2 copy-start.31
  978.1 1.1 copy-start.32
  978.6 1.1 copy-start.29
  979.2 1.1 copy-start.28
  980.8 1.1 copy-start.7
  980.8 1.4 copy-start.10
  982.3 1.6 copy-start.41
  983.9 1.4 copy-start.40
  983.9 1.6 copy-start.39
  985.3 1.3 copy-start.38
  985.5 2.0 copy-start.37
  986.6 1.2 copy-start.36
  987.6 1.1 copy-start.35
  988.8 4.1 copy-start.43
  990.2 4.1 copy-start.42
  992.9 4.1 copy-start.4
  992.9 4.1 copy-start.45
Sparse Core Ops, SparseCore 0:
  69.0 69.3 reduce-scatter.13
  277.6 110.5 all-reduce.24
  391.5 83.0 all-reduce.30
  477.3 33.5 all-reduce.26
  533.9 164.3 all-reduce.28
  714.2 85.8 all-reduce.32
  835.4 68.1 reduce-scatter.15
  976.2 26.1 all-reduce.34
  1005.3 40.9 reduce-scatter.17
